TPU v7x, 32 devices: a whole 2x2x4 slice. The times are simulated.
32 devices in a mesh: groups: 2 (over y), ctx: 4 (over z), fsdp: 4 (over x, core).
Axes of the slice: x: 2, y: 2, z: 4, core: 2. Of those that a mesh axis runs over, the one named last changes fastest.
Arguments:
- patches: bfloat16 [8192, 1024], P(('groups', 'ctx', 'fsdp')), parts along dimension 0, may hold values from -6 to 6
- labels: int32 [8192], P(('groups', 'ctx', 'fsdp')), parts along dimension 0, may hold values from 0 to 127
- op_ids: int32 [4, 3], P('groups'), parts along dimension 0, may hold values from 0 to 8
- mix_codes: int32 [4, 4], P('groups'), parts along dimension 0, may hold values from 1 to 8
- aug_gains: float32 [9, 1024], replicated, may hold values from 0.1 to 1.9
- in_weight: bfloat16 [1024, 1536], P('fsdp'), may hold values from -0.1875 to 0.1875
- dt_weight: bfloat16 [1024, 32], P('fsdp'), may hold values from -0.09375 to 0.09375
- dt_bias: float32 [2, 16], replicated, may hold values from -3.9 to -2.2
- decay_log: float32 [2, 16], replicated, may hold values from -12 to 0
- skip_gain: float32 [16], replicated, may hold values from 0.1 to 1.9
- norm_gain: float32 [1024], replicated, may hold values from 0.5 to 1.5
- out_weight: bfloat16 [1024, 1024], P('fsdp'), may hold values from -0.1875 to 0.1875
- head_weight: bfloat16 [1024, 128], replicated, may hold values from -8 to 8
Outputs:
- grad_out: float32 [2048, 1024], P(('groups', 'ctx', 'fsdp')), parts along dimension 0
- grad_head: float32 [2048, 128], P(('groups', 'ctx', 'fsdp')), parts along dimension 0
- patch_loss: float32 [8192], P(('groups', 'ctx', 'fsdp')), parts along dimension 0
There are 2 independent parts, one for each index of `groups`. A program takes and returns all parts, laid end to end along the dimension named above; an argument that names none is the same for every part. Nothing has to cross between parts.
All inputs are finite; a program needn't handle non-finite values.
Results may differ from a plain program's by a relative error of at most 0.01505.
The roundings to bfloat16 on the way count: a program that leaves them out, or rounds other values in their place, can miss the bound.
Values may be sent and summed in bfloat16 or wider, within the bound.
A program may use at most 128 MiB of HBM per device.

v0:
```python
import jax
import jax.numpy as jnp
from jax import lax
from jax.sharding import PartitionSpec as P

D = 1024
HEADS = 16
HEAD_DIM = 64
STATE = 128
CLASSES = 128
VIEWS = 3
NOPS = 9
WIDTH_AUG = 3
BLOCK = 128
loss_scale = 256.0
mix_lambda = 12.0
highest = lax.Precision.HIGHEST


def carried_in_2(value, axis, combine, identity, reverse):
    count, mine = (lax.axis_size(axis), lax.axis_index(axis))
    everything = jax.tree.map(lambda part: lax.all_gather(part, axis), value)
    start = jax.tree.map(
        lambda part, zero: jnp.broadcast_to(jnp.asarray(zero, part.dtype), part.shape),
        value,
        identity,
    )

    def turn(k, before):
        at = count - 1 - k if reverse else k
        reached = at > mine if reverse else at < mine
        new = combine(before, jax.tree.map(lambda part: part[at], everything))
        return jax.tree.map(lambda a, b: jnp.where(reached, a, b), new, before)

    return lax.fori_loop(0, count, turn, start)


def view_scales(op_ids, mix_codes, aug_gains):
    code_values = mix_codes.astype(jnp.float32)
    weights = code_values[:, :WIDTH_AUG] / jnp.sum(
        code_values[:, :WIDTH_AUG], axis=1, keepdims=True
    )
    keep_share = code_values[:, WIDTH_AUG] / 9.0
    onehot = (op_ids[:, :, None] == jnp.arange(NOPS, dtype=jnp.int32)[None, None, :]).astype(
        jnp.float32
    )
    op_weights = jnp.sum(onehot * weights[:, :, None], axis=1)
    mixed_gain = jnp.dot(op_weights, aug_gains, precision=highest)
    scaled = keep_share[:, None] + (1.0 - keep_share[:, None]) * mixed_gain
    return jnp.concatenate([jnp.ones((1, D), jnp.float32), scaled], axis=0)


def block_pass(values, write_vectors, read_vectors, step_sizes, decay_rates):
    length, head_count, head_width = values.shape
    pieces = length // BLOCK
    shaped = (
        values.reshape(pieces, BLOCK, head_count, head_width),
        write_vectors.reshape(pieces, BLOCK, STATE),
        read_vectors.reshape(pieces, BLOCK, STATE),
        step_sizes.reshape(pieces, BLOCK, head_count),
    )
    lower_mask = jnp.arange(BLOCK)[:, None] >= jnp.arange(BLOCK)[None, :]

    def advance(carried_in, inputs):
        state_now, offset = carried_in
        piece_values, piece_write, piece_read, piece_steps = inputs
        value_float = piece_values.astype(jnp.float32)
        write_float = piece_write.astype(jnp.float32)
        read_float = piece_read.astype(jnp.float32)
        step_logs = piece_steps * decay_rates[None, :]
        running = jnp.cumsum(step_logs, axis=0)
        log_gaps = running[:, None, :] - running[None, :, :]
        mask_decay = jnp.exp(jnp.where(lower_mask[:, :, None], log_gaps, -1e30))
        scores = jnp.dot(read_float, write_float.T, precision=highest)
        mixing = scores[:, :, None] * mask_decay * piece_steps[None, :, :]
        inside = jnp.einsum("tsh,shp->thp", mixing, value_float, precision=highest)
        carried = jnp.exp(running)[:, :, None] * jnp.einsum(
            "tn,hpn->thp", read_float, state_now, precision=highest
        )
        last_log = running[-1]
        weighted = (jnp.exp(last_log[None, :] - running) * piece_steps)[:, :, None] * value_float
        new_state = jnp.exp(last_log)[:, None, None] * state_now + jnp.einsum(
            "shp,sn->hpn", weighted, write_float, precision=highest
        )
        return ((new_state, offset + last_log), (inside + carried, offset[None, :] + running))

    initial = (
        jnp.zeros((head_count, head_width, STATE), jnp.float32),
        jnp.zeros((head_count,), jnp.float32),
    )
    (final_state, total_log), (outputs, positions_log) = lax.scan(advance, initial, shaped)
    return (
        outputs.reshape(length, head_count, head_width),
        positions_log.reshape(length, head_count),
        final_state,
        total_log,
    )


def loss_terms(logits, labels):
    log_probs = jax.nn.log_softmax(logits, axis=-1)
    probabilities = jnp.exp(log_probs)
    log_mean = jax.scipy.special.logsumexp(log_probs, axis=0) - jnp.log(jnp.float32(VIEWS))
    spread = jnp.sum(probabilities * (log_probs - log_mean[None]), axis=(0, 2)) / VIEWS
    onehot = (labels[:, None] == jnp.arange(CLASSES, dtype=jnp.int32)[None, :]).astype(jnp.float32)
    cross_entropy = -jnp.sum(onehot * log_probs[0], axis=-1)
    return cross_entropy + mix_lambda * spread


def combine_states(earlier, later):
    earlier_log, earlier_state = earlier
    later_log, later_state = later
    return (
        earlier_log + later_log,
        jnp.exp(later_log)[:, :, None, None] * earlier_state + later_state,
    )


def apply_incoming(outputs, positions_log, read_vectors, incoming):
    reached = jnp.einsum(
        "vtn,vhpn->vthp", read_vectors.astype(jnp.float32), incoming, precision=highest
    )
    return outputs + jnp.exp(positions_log)[:, :, :, None] * reached


def on_device(
    patches,
    labels,
    op_ids,
    mix_codes,
    aug_gains,
    in_weight,
    dt_weight,
    dt_bias,
    decay_log,
    skip_gain,
    norm_gain,
    out_weight,
    head_weight,
):
    row_count = patches.shape[0]
    ctx_count = lax.axis_size("ctx")
    fsdp_count = lax.axis_size("fsdp")
    fsdp_place = lax.axis_index("fsdp")
    total_patches = row_count * ctx_count * fsdp_count
    inner_width = out_weight.shape[0] * fsdp_count
    local_heads = HEADS // fsdp_count
    range_rows = row_count * fsdp_count
    scales = view_scales(op_ids, mix_codes, aug_gains)
    views = (scales[:, None, :] * patches.astype(jnp.float32)[None]).astype(jnp.bfloat16)
    flat_rows = views.reshape(VIEWS * row_count, D)
    columns = flat_rows
    proj_sum = jnp.dot(
        columns,
        lax.all_gather(in_weight, "fsdp", axis=0, tiled=True),
        preferred_element_type=jnp.float32,
    )
    raw_sum = jnp.dot(
        columns,
        lax.all_gather(dt_weight, "fsdp", axis=0, tiled=True),
        preferred_element_type=jnp.float32,
    )
    projected = proj_sum.astype(jnp.bfloat16).reshape(VIEWS, row_count, in_weight.shape[1])
    step_sizes = jax.nn.softplus(raw_sum.reshape(VIEWS, row_count, 2, HEADS) + dt_bias[None, None])
    value_rows = projected[:, :, :inner_width].reshape(
        VIEWS, row_count, fsdp_count, local_heads * HEAD_DIM
    )
    head_rows = lax.all_to_all(value_rows, "fsdp", split_axis=2, concat_axis=1, tiled=True)
    values = head_rows.reshape(VIEWS, range_rows, local_heads, HEAD_DIM)
    step_rows = step_sizes.reshape(VIEWS, row_count, 2, fsdp_count, local_heads)
    head_step_rows = lax.all_to_all(step_rows, "fsdp", split_axis=3, concat_axis=1, tiled=True)
    local_steps = head_step_rows.reshape(VIEWS, range_rows, 2, local_heads)
    shared = lax.all_gather(projected[:, :, inner_width:], "fsdp", axis=1, tiled=True)
    coefficients = shared.reshape(VIEWS, range_rows, 4, STATE)
    head_start = fsdp_place * local_heads
    decay_rates = lax.dynamic_slice_in_dim(-jnp.exp(decay_log), head_start, local_heads, 1)
    local_skip = lax.dynamic_slice_in_dim(skip_gain, head_start, local_heads, 0)
    local_gain = lax.dynamic_slice_in_dim(
        norm_gain, head_start * HEAD_DIM, local_heads * HEAD_DIM, 0
    )
    mapped = jax.vmap(block_pass, in_axes=(0, 0, 0, 0, None))
    forward_read = coefficients[:, :, 1]
    forward_out, forward_logs, forward_state, forward_total = mapped(
        values, coefficients[:, :, 0], forward_read, local_steps[:, :, 0], decay_rates[0]
    )
    reverse_values = jnp.flip(values, 1)
    reverse_read = jnp.flip(coefficients[:, :, 3], 1)
    reverse_out, reverse_logs, reverse_state, reverse_total = mapped(
        reverse_values,
        jnp.flip(coefficients[:, :, 2], 1),
        reverse_read,
        jnp.flip(local_steps[:, :, 1], 1),
        decay_rates[1],
    )
    identity = (jnp.zeros_like(forward_total), jnp.zeros_like(forward_state))
    forward_in = carried_in_2(
        (forward_total, forward_state), "ctx", combine_states, identity, False
    )
    reverse_in = carried_in_2((reverse_total, reverse_state), "ctx", combine_states, identity, True)
    forward_full = apply_incoming(forward_out, forward_logs, forward_read, forward_in[1])
    reverse_full = apply_incoming(reverse_out, reverse_logs, reverse_read, reverse_in[1])
    mixed = (
        forward_full
        + jnp.flip(reverse_full, 1)
        + local_skip[None, None, :, None] * values.astype(jnp.float32)
    )
    mixed = mixed.reshape(VIEWS, range_rows, local_heads * HEAD_DIM)
    square_total = lax.psum(jnp.sum(mixed * mixed, axis=-1), "fsdp")
    scaling = lax.rsqrt(square_total / inner_width + 1e-05)
    normed_heads = (mixed * scaling[:, :, None] * local_gain[None, None, :]).astype(jnp.bfloat16)
    normed_rows = lax.all_to_all(normed_heads, "fsdp", split_axis=1, concat_axis=2, tiled=True)
    normed = normed_rows.reshape(VIEWS * row_count, inner_width)
    columns = normed
    out_sum = jnp.dot(
        columns,
        lax.all_gather(out_weight, "fsdp", axis=0, tiled=True),
        preferred_element_type=jnp.float32,
    )
    hidden = (flat_rows.astype(jnp.float32) + out_sum).astype(jnp.bfloat16)
    logits = jnp.dot(hidden, head_weight, preferred_element_type=jnp.float32).reshape(
        VIEWS, row_count, CLASSES
    )

    def per_patch(logit_values):
        return loss_terms(logit_values, labels)

    patch_loss, pullback = jax.vjp(per_patch, logits)
    (grad_logits,) = pullback(jnp.full((row_count,), loss_scale / total_patches, jnp.float32))
    grad_logits_bf = grad_logits.reshape(VIEWS * row_count, CLASSES).astype(jnp.bfloat16)
    grad_hidden = lax.dot_general(
        grad_logits_bf, head_weight, (((1,), (1,)), ((), ())), preferred_element_type=jnp.float32
    ).astype(jnp.bfloat16)
    head_term = lax.dot_general(
        hidden, grad_logits_bf, (((0,), (0,)), ((), ())), preferred_element_type=jnp.float32
    )
    columns = normed
    grad_out = lax.psum_scatter(
        lax.dot_general(
            columns, grad_hidden, (((0,), (0,)), ((), ())), preferred_element_type=jnp.float32
        ),
        ("ctx", "fsdp"),
        scatter_dimension=0,
        tiled=True,
    )
    grad_head = lax.psum_scatter(head_term, ("ctx", "fsdp"), scatter_dimension=0, tiled=True)
    return (grad_out, grad_head, patch_loss)


def solution(mesh):
    return jax.shard_map(
        on_device,
        mesh=mesh,
        in_specs=(
            P(("groups", "ctx", "fsdp"), None),
            P(("groups", "ctx", "fsdp")),
            P("groups", None),
            P("groups", None),
            P(),
            P("fsdp", None),
            P("fsdp", None),
            P(),
            P(),
            P(),
            P(),
            P("fsdp", None),
            P(),
        ),
        out_specs=(
            P(("groups", "ctx", "fsdp"), None),
            P(("groups", "ctx", "fsdp"), None),
            P(("groups", "ctx", "fsdp")),
        ),
        check_vma=False,
    )
```

profile of v0, /device:TPU:0, one launch (start us, length us, event | category | flops | bytes accessed | tf_op | source)
XLA Modules:
  0.0 552.4 jit_solution(7558193707011760850)
XLA Ops:
  11.7 29.2 %all-gather.12.cloned.1.call-done = bf16[1024,1536]{1,0:T(8,128)(2,1)} async-done(((bf16[256,1536]{1,0:T(8,128)(2,1)}), bf16[1024,1536]{1,0:T(8,128)(2,1)}) %all-gather.12.cloned.1.call-update) | async-done | bytes 3145744 | tf_op jit(solution)/shard_map/all_gather | solution.py:155
  40.8 4.7 convolution_convert_fusion
  48.3 5.2 all_gather.36
  54.9 3.3 all-to-all-start
  63.8 3.6 all-to-all-start.1
  68.5 24.8 %all-to-all-done.1 = bf16[3,256,4,256]{1,3,0,2:T(8,128)(2,1)S(1)} async-done(((bf16[3,256,4,256]{1,3,0,2:T(8,128)(2,1)}), bf16[3,256,4,256]{1,3,0,2:T(8,128)(2,1)S(1)}, u32[]{:S(2)}, u32[]{:S(2)}) %all-to-all-start.1) | async-done | bytes 1572896 | tf_op jit(solution)/shard_map/all_to_all | solution.py:168
  98.5 3.6 reshape_reshape.3
  102.2 3.7 rev.20
  105.9 3.1 copy.256
  110.7 3.6 fusion.116
  114.3 10.3 %rev.22 = bf16[3,1024,128]{1,2,0:T(8,128)(2,1)S(1)} reverse(bf16[3,1024,128]{1,2,0:T(8,128)(2,1)} %get-tuple-element.680), dimensions={1} | reverse | bytes 1572864 | tf_op jit(solution)/shard_map/jit(_flip)/rev | solution.py:187
  128.2 10.3 %rev.21 = bf16[3,1024,128]{1,2,0:T(8,128)(2,1)S(1)} reverse(bf16[3,1024,128]{1,2,0:T(8,128)(2,1)} %get-tuple-element.681), dimensions={1} | reverse | bytes 1572864 | tf_op jit(solution)/shard_map/jit(_flip)/rev | solution.py:190
  145.5 72.5 %while.66 = (s32[]{:T(128)}, f32[3,4,64,128]{3,2,1,0:T(8,128)S(1)}, f32[3,4]{1,0:T(4,128)S(1)}, f32[8,3,128,4,64]{2,4,3,1,0:T(8,128)}, f32[8,3,128,4]{3,2,1,0:T(...) while((s32[]{:T(128)}, f32[3,4,64,128]{3,2,1,0:T(8,128)S(1)}, ...), condition=%wide.region_9.10_spmd.clone, body=%wide.region_7.9_spmd.clone.sunk | while | flops 467358240 | bytes 3932897 | solution.py:91
  185.6 2.9 fusion.193
  194.7 2.9 fusion.193
  203.8 2.9 fusion.193
  212.8 2.9 fusion.193
  230.4 65.1 %while.64 = (s32[]{:T(128)}, f32[3,4,64,128]{3,2,1,0:T(8,128)S(1)}, f32[3,4]{1,0:T(4,128)S(1)}, f32[8,3,128,4,64]{2,4,3,1,0:T(8,128)}, f32[8,3,128,4]{3,2,1,0:T(...) while((s32[]{:T(128)}, f32[3,4,64,128]{3,2,1,0:T(8,128)S(1)}, ...), condition=%wide.region_4.5_spmd.clone, body=%wide.region_2.4_spmd.clone.sunk | while | flops 467358240 | bytes 3932897 | solution.py:91
  297.7 12.0 %all-gather.5 = f32[4,3,4]{2,1,0:T(4,128)S(1)} all-gather(f32[1,3,4]{2,1,0:T(4,128)S(1)} %bitcast.380), channel_id=4, replica_groups=mesh['groups'=2,'ctx'=4,'fsdp'=4] {'ctx'}, dimensions={0}, use_global_device_ids=true | all-gather | bytes 240 | tf_op jit(solution)/shard_map/all_gather | solution.py:22
  314.4 12.2 %all-gather.4 = f32[4,3,4]{2,1,0:T(4,128)S(1)} all-gather(f32[1,3,4]{2,1,0:T(4,128)S(1)} %bitcast.379), channel_id=2, replica_groups=mesh['groups'=2,'ctx'=4,'fsdp'=4] {'ctx'}, dimensions={0}, use_global_device_ids=true | all-gather | bytes 240 | tf_op jit(solution)/shard_map/all_gather | solution.py:22
  331.4 4.7 while.67
  336.1 5.0 bitcast_add_fusion.4
  341.2 6.7 %rev.23 = f32[3,1024,4,64]{1,3,2,0:T(8,128)} reverse(f32[3,1024,4,64]{1,3,2,0:T(8,128)} %bitcast_add_fusion.4), dimensions={1} | reverse | bytes 6291456 | tf_op jit(solution)/shard_map/jit(_flip)/rev | solution.py:204
  347.8 4.6 while.65
  352.4 6.9 %multiply_reduce_fusion = (f32[3,1024]{1,0:T(4,128)S(1)}, f32[3,1024,4,64]{1,3,2,0:T(8,128)}) fusion(bf16[3,1024,4,64]{1,3,2,0:T(8,128)(2,1)S(1)} %reshape.248, f32[4]{0:T(128)S(1)} %dynamic_slice.71, f32[3,1024,4,64]{1,3,2,0:T(8,128)} %rev.23, f32[3,4,64,128]{3,2,1,0:T(8,128)S(1)} %get-tuple-element.353, bf16[3,1024,4,128]{1,3,2,0:T(8,128)(2,1)} %bitcast.353, ...), kind=kOutput, calls=%fused_computation.119 | convolution fusion | flops 1214247936 | bytes 12251152 | tf_op jit(solution)/shard_map/vtn,vhpn->vthp/dot_general | solution.py:120
  361.7 10.4 %psum.7 = f32[3,1024]{1,0:T(4,128)S(1)} all-reduce(f32[3,1024]{1,0:T(4,128)S(1)} %get-tuple-element.690), channel_id=1, replica_groups=mesh['groups'=2,'ctx'=4,'fsdp'=4] {'fsdp'}, use_global_device_ids=true, to_apply=%region_13.14 | all-reduce | flops 3072 | bytes 24576 | tf_op jit(solution)/shard_map/psum | solution.py:208
  375.3 3.7 all-to-all-start.2
  379.4 25.3 %all-to-all-done.2 = bf16[3,1024,256]{2,0,1:T(4,128)(2,1)S(1)} async-done(((bf16[3,1024,256]{2,0,1:T(4,128)(2,1)}), bf16[3,1024,256]{2,0,1:T(4,128)(2,1)S(1)}, u32[]{:S(2)}, u32[]{:S(2)}) %all-to-all-start.2) | async-done | bytes 1572896 | tf_op jit(solution)/shard_map/all_to_all | solution.py:211
  407.7 4.3 add_convert_fusion
  416.0 5.6 %fusion.94 = f32[1024,1024]{1,0:T(8,128)} fusion(bf16[768,1024]{1,0:T(8,128)(2,1)} %bitcast.371, bf16[768,128]{1,0:T(8,128)(2,1)S(1)} %bitcast.373, bf16[1024,128]{1,0:T(8,128)(2,1)S(1)} %copy-done), kind=kOutput, calls=%fused_computation.127 | convolution fusion | flops 1812725760 | bytes 6225920 | tf_op jit(solution)/shard_map/dot_general | solution.py:238
  422.8 46.5 %reduce-scatter.5.cloned.1.call-done = f32[64,128]{1,0:T(8,128)} async-done(((f32[1024,128]{1,0:T(8,128)}), f32[64,128]{1,0:T(8,128)}) %reduce-scatter.5.cloned.1.call-update) | async-done | bytes 32784 | tf_op jit(solution)/shard_map/reduce_scatter | solution.py:245
  469.3 76.3 %reduce-scatter.3.cloned.1.call-done = f32[64,1024]{1,0:T(8,128)} async-done(((f32[1024,1024]{1,0:T(8,128)}), f32[64,1024]{1,0:T(8,128)}) %reduce-scatter.3.cloned.1.call-update) | async-done | bytes 262160 | tf_op jit(solution)/shard_map/reduce_scatter | solution.py:237
  (433 shorter events, 204.7 us)
Async XLA Ops:
  7.2 404.8 %copy-start = (bf16[1024,128]{1,0:T(8,128)(2,1)S(1)}, bf16[1024,128]{1,0:T(8,128)(2,1)}, u32[]{:S(2)}) copy-start(bf16[1024,128]{1,0:T(8,128)(2,1)} %param.33) | copy-start | bytes 786436
  7.2 4.0 copy-start.12
  7.2 33.7 %all-gather.12.cloned.1.call-start = ((), (), s32[]{:S(2)}) async-start(), calls=%async_computation.5 | async-start | bytes 3932160 | tf_op jit(solution)/shard_map/all_gather | solution.py:155
  7.9 102.7 %all-gather.14.cloned.1.call-start = ((), (), s32[]{:S(2)}) async-start(), calls=%async_computation.6 | async-start | bytes 3932160 | tf_op jit(solution)/shard_map/all_gather | solution.py:173
  11.7 33.9 %copy-start.8 = (bf16[3,256,1024]{2,1,0:T(8,128)(2,1)}, bf16[3,256,1024]{2,1,0:T(8,128)(2,1)S(1)}, u32[]{:S(2)}) copy-start(bf16[3,256,1024]{2,1,0:T(8,128)(2,1)S(1)} %multiply_convert_fusion.1) | copy-start | bytes 4718596
  45.5 1.4 copy-start.7
  47.0 1.3 copy-start.9
  47.0 6.5 %copy-start.13 = (f32[2,16]{1,0:T(2,128)S(1)}, f32[2,16]{1,0:T(2,128)}, u32[]{:S(2)}) copy-start(f32[2,16]{1,0:T(2,128)} %param.28) | copy-start | bytes 388
  54.9 8.9 %all-to-all-start = ((f32[3,256,2,4,4]{1,4,2,0,3:T(4,128)}), f32[3,256,2,4,4]{1,4,2,0,3:T(4,128)S(1)}, u32[]{:S(2)}, u32[]{:S(2)}) async-start(f32[3,256,2,4,4]{1,4,2,0,3:T(4,128)} %copy.246), calls=%async_computation | async-start | bytes 196608 | tf_op jit(solution)/shard_map/all_to_all | solution.py:171
  61.7 5.8 %copy-start.11 = (f32[2,16]{1,0:T(2,128)S(1)}, f32[2,16]{1,0:T(2,128)}, u32[]{:S(2)}) copy-start(f32[2,16]{1,0:T(2,128)} %param.29) | copy-start | bytes 388
  63.8 29.5 %all-to-all-start.1 = ((bf16[3,256,4,256]{1,3,0,2:T(8,128)(2,1)}), bf16[3,256,4,256]{1,3,0,2:T(8,128)(2,1)S(1)}, u32[]{:S(2)}, u32[]{:S(2)}) async-start(bf16[3,256,4,256]{1,3,0,2:T(8,128)(2,1)} %copy.249), calls=%async_computation.1 | async-start | bytes 3145728 | tf_op jit(solution)/shard_map/all_to_all | solution.py:168
  67.4 264.0 %all-gather.20.cloned.1.call-start = ((), (), s32[]{:S(2)}) async-start(), calls=%async_computation.11 | async-start | bytes 1966080 | tf_op jit(solution)/shard_map/all_gather | solution.py:22
  105.9 3.1 copy-start.5
  124.6 3.6 copy-start.3
  217.9 0.7 copy-start.2
  218.7 129.1 %all-gather.18.cloned.1.call-start = ((), (), s32[]{:S(2)}) async-start(), calls=%async_computation.10 | async-start | bytes 1966080 | tf_op jit(solution)/shard_map/all_gather | solution.py:22
  218.9 4.7 copy-start.6
  230.4 66.5 %copy-start.14 = (f32[16]{0:T(128)S(1)}, f32[16]{0:T(128)}, u32[]{:S(2)}) copy-start(f32[16]{0:T(128)} %param.30) | copy-start | bytes 196
  295.5 0.8 copy-start.1
  296.3 111.4 %all-gather.16.cloned.1.call-start = ((), (), s32[]{:S(2)}) async-start(), calls=%async_computation.7 | async-start | bytes 2621440 | tf_op jit(solution)/shard_map/all_gather | solution.py:216
  331.4 4.8 copy-start.4
  375.3 4.0 copy-start.10
  375.3 29.4 %all-to-all-start.2 = ((bf16[3,1024,256]{2,0,1:T(4,128)(2,1)}), bf16[3,1024,256]{2,0,1:T(4,128)(2,1)S(1)}, u32[]{:S(2)}, u32[]{:S(2)}) async-start(bf16[3,1024,256]{2,0,1:T(4,128)(2,1)} %copy.268), calls=%async_computation.2 | async-start | bytes 4194304 | tf_op jit(solution)/shard_map/all_to_all | solution.py:211
  379.0 90.3 %reduce-scatter.5.cloned.1.call-start = ((), (), s32[]{:S(2)}) async-start(), calls=%async_computation.9 | async-start | bytes 557056 | tf_op jit(solution)/shard_map/reduce_scatter | solution.py:245
  415.9 129.6 %reduce-scatter.3.cloned.1.call-start = ((), (), s32[]{:S(2)}) async-start(), calls=%async_computation.8 | async-start | bytes 4456448 | tf_op jit(solution)/shard_map/reduce_scatter | solution.py:237
Sparse Core Ops, SparseCore 0:
  9.6 31.2 all-gather.11
  48.4 35.9 all-gather.13
  218.8 37.0 all-gather.19
  296.4 37.3 all-gather.17
  335.2 21.4 all-gather.15
  416.1 53.1 reduce-scatter.4
  474.2 71.3 reduce-scatter.2
where the time goes:
time: 558 us; the launch traced here: 552 us
  waiting for transfers between devices  205 us (37%)
  matrix products  141 us (25%)
  local copies, waits for them, and re-layouts  107 us (19%)
  blocking collectives  39.8 us (7%)
  other arithmetic  32.1 us (6%)
  between operations  14.7 us (3%)
  starting transfers between devices  11.3 us (2%)
    reduce_scatter x1, waiting for transfers between devices, on_device(): lax.psum_scatter(lax.dot_general(columns, grad_hidden, (((0,), (0,)), (()...  76.3 us
    reduce_scatter x1, waiting for transfers between devices, on_device(): lax.psum_scatter(head_term, ('ctx', 'fsdp'), scatter_dimension=0, tiled=T...  46.5 us
    dot_general x16, matrix products, advance(): inside = jnp.einsum('tsh,shp->thp', mixing, value_float, precision=highest)  44.6 us
    all_gather x1, waiting for transfers between devices, on_device(): lax.all_gather(in_weight, 'fsdp', axis=0, tiled=True)  29.2 us
    dot_general x16, matrix products, advance(): jnp.einsum('tn,hpn->thp', read_float, state_now, precision=highest)  26 us
    all_to_all x1, waiting for transfers between devices, on_device(): lax.all_to_all(normed_heads, 'fsdp', split_axis=1, concat_axis=2, tiled=T...  25.3 us
    all_to_all x1, waiting for transfers between devices, on_device(): lax.all_to_all(value_rows, 'fsdp', split_axis=2, concat_axis=1, tiled=True)  24.8 us
    all_gather x2, blocking collectives, carried_in_2(): everything = jax.tree.map(lambda part: lax.all_gather(part, axis), value)  24.2 us
  transfers between devices with their start and end apart: 10, of which 6 were waited for; matrix products, arithmetic and copies ran while one was open for 28% of the time, Pallas kernels for 0%

commit v1 on v0

--- a/solution.py
+++ b/solution.py
@@ -15,6 +15,18 @@
 loss_scale = 256.0
 mix_lambda = 12.0
 highest = lax.Precision.HIGHEST
+
+
+def register_page_now(frame_in, axis_no, x_local):
+    z2 = frame_in.shape
+    piece_now = frame_in.reshape(*z2[:axis_no], x_local, z2[axis_no] // x_local, *z2[axis_no + 1 :])
+    return jnp.moveaxis(piece_now, axis_no, 0)
+
+
+def _update_desk(my_data, along_dim):
+    res = list(my_data.shape[1:])
+    res[along_dim] *= my_data.shape[0]
+    return jnp.moveaxis(my_data, 0, along_dim).reshape(res)
 
 
 def carried_in_2(value, axis, combine, identity, reverse):
@@ -208,7 +220,20 @@
     square_total = lax.psum(jnp.sum(mixed * mixed, axis=-1), "fsdp")
     scaling = lax.rsqrt(square_total / inner_width + 1e-05)
     normed_heads = (mixed * scaling[:, :, None] * local_gain[None, None, :]).astype(jnp.bfloat16)
-    normed_rows = lax.all_to_all(normed_heads, "fsdp", split_axis=1, concat_axis=2, tiled=True)
+    x_new = lax.axis_size("fsdp")
+    main = lax.axis_index("fsdp")
+    local_next, value_now = (x_new, main)
+    tmp = register_page_now(normed_heads, 1, local_next)
+    pool = [tmp[value_now]]
+    for nth in range(1, local_next):
+        newest = tmp[(value_now + nth) % local_next]
+        front = lax.ppermute(
+            newest, "fsdp", [(p, (p + nth) % local_next) for p in range(local_next)]
+        )
+        pool.append(front)
+    q_next = jnp.stack(pool, 0)
+    tmp = q_next[(value_now - jnp.arange(local_next)) % local_next]
+    normed_rows = _update_desk(tmp, 2)
     normed = normed_rows.reshape(VIEWS * row_count, inner_width)
     columns = normed
     out_sum = jnp.dot(

time: 558 us -> 558 us (level)
  local copies, waits for them, and re-layouts: 107 us -> 118 us
  waiting for transfers between devices: 205 us -> 194 us
    all_to_all x1 -> x0, waiting for transfers between devices: 25.3 us -> none  [on_device(): lax.all_to_all(normed_heads, 'fsdp', split_axis=1, concat_axis=2, tiled=T...]
    ppermute x0 -> x3, waiting for transfers between devices: none -> 15.8 us  [on_device(): lax.ppermute(newest, 'fsdp', [(p, (p + nth) % local_next) for p in range(...]
    reshape x1 -> x2, local copies, waits for them, and re-layouts: 2.37 us -> 10 us  [on_device(): mixed = mixed.reshape(VIEWS, range_rows, local_heads * HEAD_DIM)]
    unnamed x39 -> x37, local copies, waits for them, and re-layouts: 16 us -> 17 us
  transfers between devices with their start and end apart: 10 -> 12, of which waited for: 6 -> 7; matrix products, arithmetic and copies ran while one was open for 28% -> 31% of each run, Pallas kernels for 0% -> 0%
where the time goes in v1:
time: 558 us; the launch traced here: 553 us
  waiting for transfers between devices  194 us (35%)
  matrix products  141 us (25%)
  local copies, waits for them, and re-layouts  118 us (21%)
  blocking collectives  39.6 us (7%)
  other arithmetic  35.4 us (6%)
  between operations  14.7 us (3%)
  starting transfers between devices  9.4 us (2%)
    reduce_scatter x1, waiting for transfers between devices, on_device(): lax.psum_scatter(lax.dot_general(columns, grad_hidden, (((0,), (0,)), (()...  76.3 us
    reduce_scatter x1, waiting for transfers between devices, on_device(): lax.psum_scatter(head_term, ('ctx', 'fsdp'), scatter_dimension=0, tiled=T...  48.3 us
    dot_general x16, matrix products, advance(): inside = jnp.einsum('tsh,shp->thp', mixing, value_float, precision=highest)  44.6 us
    all_gather x1, waiting for transfers between devices, on_device(): lax.all_gather(in_weight, 'fsdp', axis=0, tiled=True)  28 us
    dot_general x16, matrix products, advance(): jnp.einsum('tn,hpn->thp', read_float, state_now, precision=highest)  26 us
    all_to_all x1, waiting for transfers between devices, on_device(): lax.all_to_all(value_rows, 'fsdp', split_axis=2, concat_axis=1, tiled=True)  24.5 us
    all_gather x2, blocking collectives, carried_in_2(): everything = jax.tree.map(lambda part: lax.all_gather(part, axis), value)  24.1 us
    dot_general x16, matrix products, advance(): jnp.einsum('shp,sn->hpn', weighted, write_float, precision=highest)  22.5 us
  transfers between devices with their start and end apart: 12, of which 7 were waited for; matrix products, arithmetic and copies ran while one was open for 31% of the time, Pallas kernels for 0%

profile of v1, /device:TPU:0, one launch (start us, length us, event | category | flops | bytes accessed | tf_op | source)
XLA Modules:
  0.0 553.1 jit_solution(4162645939532604132)
XLA Ops:
  12.9 28.0 %all-gather.12.cloned.1.call-done = bf16[1024,1536]{1,0:T(8,128)(2,1)} async-done(((bf16[256,1536]{1,0:T(8,128)(2,1)}), bf16[1024,1536]{1,0:T(8,128)(2,1)}) %all-gather.12.cloned.1.call-update) | async-done | bytes 3145744 | tf_op jit(solution)/shard_map/all_gather | solution.py:167
  40.8 5.0 convolution_convert_fusion
  48.6 5.2 all_gather.36
  55.1 3.3 all-to-all-start
  64.3 3.7 all-to-all-start.1
  69.1 24.5 %all-to-all-done.1 = bf16[3,256,4,256]{1,3,0,2:T(8,128)(2,1)S(1)} async-done(((bf16[3,256,4,256]{1,3,0,2:T(8,128)(2,1)}), bf16[3,256,4,256]{1,3,0,2:T(8,128)(2,1)S(1)}, u32[]{:S(2)}, u32[]{:S(2)}) %all-to-all-start.1) | async-done | bytes 1572896 | tf_op jit(solution)/shard_map/all_to_all | solution.py:180
  98.9 3.6 reshape_reshape.6
  102.5 3.7 rev.20
  106.2 3.1 copy.148
  110.9 3.6 fusion.118
  114.6 10.3 %rev.22 = bf16[3,1024,128]{1,2,0:T(8,128)(2,1)S(1)} reverse(bf16[3,1024,128]{1,2,0:T(8,128)(2,1)} %get-tuple-element.620), dimensions={1} | reverse | bytes 1572864 | tf_op jit(solution)/shard_map/jit(_flip)/rev | solution.py:199
  128.5 10.3 %rev.21 = bf16[3,1024,128]{1,2,0:T(8,128)(2,1)S(1)} reverse(bf16[3,1024,128]{1,2,0:T(8,128)(2,1)} %get-tuple-element.621), dimensions={1} | reverse | bytes 1572864 | tf_op jit(solution)/shard_map/jit(_flip)/rev | solution.py:202
  145.8 72.5 %while.66 = (s32[]{:T(128)}, f32[3,4,64,128]{3,2,1,0:T(8,128)S(1)}, f32[3,4]{1,0:T(4,128)S(1)}, f32[8,3,128,4,64]{2,4,3,1,0:T(8,128)}, f32[8,3,128,4]{3,2,1,0:T(...) while((s32[]{:T(128)}, f32[3,4,64,128]{3,2,1,0:T(8,128)S(1)}, ...), condition=%wide.region_9.10_spmd.clone, body=%wide.region_7.9_spmd.clone.sunk | while | flops 467358240 | bytes 3932897 | solution.py:103
  195.0 2.9 fusion.195
  204.1 2.9 fusion.195
  230.7 65.2 %while.64 = (s32[]{:T(128)}, f32[3,4,64,128]{3,2,1,0:T(8,128)S(1)}, f32[3,4]{1,0:T(4,128)S(1)}, f32[8,3,128,4,64]{2,4,3,1,0:T(8,128)}, f32[8,3,128,4]{3,2,1,0:T(...) while((s32[]{:T(128)}, f32[3,4,64,128]{3,2,1,0:T(8,128)S(1)}, ...), condition=%wide.region_4.5_spmd.clone, body=%wide.region_2.4_spmd.clone.sunk | while | flops 467358240 | bytes 3932897 | solution.py:103
  298.2 12.0 %all-gather.5 = f32[4,3,4]{2,1,0:T(4,128)S(1)} all-gather(f32[1,3,4]{2,1,0:T(4,128)S(1)} %bitcast.397), channel_id=4, replica_groups=mesh['groups'=2,'ctx'=4,'fsdp'=4] {'ctx'}, dimensions={0}, use_global_device_ids=true | all-gather | bytes 240 | tf_op jit(solution)/shard_map/all_gather | solution.py:34
  315.0 12.1 %all-gather.4 = f32[4,3,4]{2,1,0:T(4,128)S(1)} all-gather(f32[1,3,4]{2,1,0:T(4,128)S(1)} %bitcast.396), channel_id=2, replica_groups=mesh['groups'=2,'ctx'=4,'fsdp'=4] {'ctx'}, dimensions={0}, use_global_device_ids=true | all-gather | bytes 240 | tf_op jit(solution)/shard_map/all_gather | solution.py:34
  331.8 4.7 while.67
  336.5 5.0 bitcast_add_fusion.4
  341.6 6.7 %rev.23 = f32[3,1024,4,64]{1,3,2,0:T(8,128)} reverse(f32[3,1024,4,64]{1,3,2,0:T(8,128)} %bitcast_add_fusion.4), dimensions={1} | reverse | bytes 6291456 | tf_op jit(solution)/shard_map/jit(_flip)/rev | solution.py:216
  348.3 4.6 while.65
  352.9 6.9 %multiply_reduce_fusion = (f32[3,1024]{1,0:T(4,128)S(1)}, f32[3,1024,4,64]{1,3,2,0:T(8,128)}) fusion(bf16[3,1024,4,64]{1,3,2,0:T(8,128)(2,1)S(1)} %reshape.304, f32[4]{0:T(128)S(1)} %dynamic_slice.77, f32[3,1024,4,64]{1,3,2,0:T(8,128)} %rev.23, f32[3,4,64,128]{3,2,1,0:T(8,128)S(1)} %get-tuple-element.353, bf16[3,1024,4,128]{1,3,2,0:T(8,128)(2,1)} %bitcast.367, ...), kind=kOutput, calls=%fused_computation.120 | convolution fusion | flops 1214247936 | bytes 12251152 | tf_op jit(solution)/shard_map/vtn,vhpn->vthp/dot_general | solution.py:132
  359.9 5.2 reshape.309
  365.0 4.9 copy.159
  369.9 10.2 %psum.7 = f32[3,1024]{1,0:T(4,128)S(1)} all-reduce(f32[3,1024]{1,0:T(4,128)S(1)} %get-tuple-element.634), channel_id=1, replica_groups=mesh['groups'=2,'ctx'=4,'fsdp'=4] {'fsdp'}, use_global_device_ids=true, to_apply=%region_13.14 | all-reduce | flops 3072 | bytes 24576 | tf_op jit(solution)/shard_map/psum | solution.py:220
  384.7 8.8 %collective-permute-done = bf16[3,256,256]{2,1,0:T(8,128)(2,1)S(1)} collective-permute-done((bf16[3,256,256]{2,1,0:T(8,128)(2,1)S(1)}, bf16[3,256,256]{2,1,0:T(8,128)(2,1)S(1)}, u32[]{:S(2)}, u32[]{:S(2)}) %collective-permute-start) | collective-permute-done | bytes 393248 | tf_op jit(solution)/shard_map/ppermute | solution.py:230
  394.7 5.8 %collective-permute-done.2 = bf16[3,256,256]{2,1,0:T(8,128)(2,1)S(1)} collective-permute-done((bf16[3,256,256]{2,1,0:T(8,128)(2,1)S(1)}, bf16[3,256,256]{2,1,0:T(8,128)(2,1)S(1)}, u32[]{:S(2)}, u32[]{:S(2)}) %collective-permute-start.2) | collective-permute-done | bytes 393248 | tf_op jit(solution)/shard_map/ppermute | solution.py:230
  406.7 4.3 add_convert_fusion
  414.9 5.6 %fusion.94 = f32[1024,1024]{1,0:T(8,128)} fusion(bf16[768,1024]{1,0:T(8,128)(2,1)} %bitcast.385, bf16[768,128]{1,0:T(8,128)(2,1)S(1)} %bitcast.387, bf16[1024,128]{1,0:T(8,128)(2,1)S(1)} %copy-done), kind=kOutput, calls=%fused_computation.129 | convolution fusion | flops 1812725760 | bytes 6225920 | tf_op jit(solution)/shard_map/dot_general | solution.py:263
  421.7 48.3 %reduce-scatter.5.cloned.1.call-done = f32[64,128]{1,0:T(8,128)} async-done(((f32[1024,128]{1,0:T(8,128)}), f32[64,128]{1,0:T(8,128)}) %reduce-scatter.5.cloned.1.call-update) | async-done | bytes 32784 | tf_op jit(solution)/shard_map/reduce_scatter | solution.py:270
  470.0 76.3 %reduce-scatter.3.cloned.1.call-done = f32[64,1024]{1,0:T(8,128)} async-done(((f32[1024,1024]{1,0:T(8,128)}), f32[64,1024]{1,0:T(8,128)}) %reduce-scatter.3.cloned.1.call-update) | async-done | bytes 262160 | tf_op jit(solution)/shard_map/reduce_scatter | solution.py:262
  (439 shorter events, 215.1 us)
Async XLA Ops:
  7.2 403.8 %copy-start = (bf16[1024,128]{1,0:T(8,128)(2,1)S(1)}, bf16[1024,128]{1,0:T(8,128)(2,1)}, u32[]{:S(2)}) copy-start(bf16[1024,128]{1,0:T(8,128)(2,1)} %param.33) | copy-start | bytes 786436
  7.2 4.0 copy-start.11
  7.2 33.7 %all-gather.12.cloned.1.call-start = ((), (), s32[]{:S(2)}) async-start(), calls=%async_computation.4 | async-start | bytes 3932160 | tf_op jit(solution)/shard_map/all_gather | solution.py:167
  7.9 103.0 %all-gather.14.cloned.1.call-start = ((), (), s32[]{:S(2)}) async-start(), calls=%async_computation.5 | async-start | bytes 3932160 | tf_op jit(solution)/shard_map/all_gather | solution.py:185
  45.8 1.4 copy-start.7
  47.3 1.3 copy-start.8
  47.3 6.5 %copy-start.12 = (f32[2,16]{1,0:T(2,128)S(1)}, f32[2,16]{1,0:T(2,128)}, u32[]{:S(2)}) copy-start(f32[2,16]{1,0:T(2,128)} %param.28) | copy-start | bytes 388
  55.1 9.1 %all-to-all-start = ((f32[3,256,2,4,4]{1,4,2,0,3:T(4,128)}), f32[3,256,2,4,4]{1,4,2,0,3:T(4,128)S(1)}, u32[]{:S(2)}, u32[]{:S(2)}) async-start(f32[3,256,2,4,4]{1,4,2,0,3:T(4,128)} %copy.138), calls=%async_computation | async-start | bytes 196608 | tf_op jit(solution)/shard_map/all_to_all | solution.py:183
  64.3 3.8 copy-start.10
  64.3 29.3 %all-to-all-start.1 = ((bf16[3,256,4,256]{1,3,0,2:T(8,128)(2,1)}), bf16[3,256,4,256]{1,3,0,2:T(8,128)(2,1)S(1)}, u32[]{:S(2)}, u32[]{:S(2)}) async-start(bf16[3,256,4,256]{1,3,0,2:T(8,128)(2,1)} %copy.141), calls=%async_computation.1 | async-start | bytes 3145728 | tf_op jit(solution)/shard_map/all_to_all | solution.py:180
  68.0 263.8 %all-gather.20.cloned.1.call-start = ((), (), s32[]{:S(2)}) async-start(), calls=%async_computation.10 | async-start | bytes 1966080 | tf_op jit(solution)/shard_map/all_gather | solution.py:34
  106.2 3.1 copy-start.5
  124.9 3.6 copy-start.3
  218.2 0.7 copy-start.2
  219.0 129.3 %all-gather.18.cloned.1.call-start = ((), (), s32[]{:S(2)}) async-start(), calls=%async_computation.9 | async-start | bytes 1966080 | tf_op jit(solution)/shard_map/all_gather | solution.py:34
  219.2 4.7 copy-start.6
  230.7 66.7 %copy-start.13 = (f32[16]{0:T(128)S(1)}, f32[16]{0:T(128)}, u32[]{:S(2)}) copy-start(f32[16]{0:T(128)} %param.30) | copy-start | bytes 196
  295.8 0.8 copy-start.1
  296.7 110.0 %all-gather.16.cloned.1.call-start = ((), (), s32[]{:S(2)}) async-start(), calls=%async_computation.6 | async-start | bytes 2621440 | tf_op jit(solution)/shard_map/all_gather | solution.py:241
  297.2 172.8 %reduce-scatter.5.cloned.1.call-start = ((), (), s32[]{:S(2)}) async-start(), calls=%async_computation.8 | async-start | bytes 557056 | tf_op jit(solution)/shard_map/reduce_scatter | solution.py:270
  331.8 4.8 copy-start.4
  382.5 2.1 copy-start.9
  382.6 10.9 %collective-permute-start = (bf16[3,256,256]{2,1,0:T(8,128)(2,1)S(1)}, bf16[3,256,256]{2,1,0:T(8,128)(2,1)S(1)}, u32[]{:S(2)}, u32[]{:S(2)}) collective-permute-start(bf16[3,256,256]{2,1,0:T(8,128)(2,1)S(1)} %get-tuple-element.626), channel_id=1, source_target_pairs={{0,1},{1,2},{2,3},{3,0},{4,5},{5,6},{6,7},{7,4},{8,9},{9,10},{10,1... | collective-permute-start | bytes 1179656 | tf_op jit(solution)/shard_map/ppermute | solution.py:230
  382.7 12.0 %collective-permute-start.1 = (bf16[3,256,256]{2,1,0:T(8,128)(2,1)S(1)}, bf16[3,256,256]{2,1,0:T(8,128)(2,1)S(1)}, u32[]{:S(2)}, u32[]{:S(2)}) collective-permute-start(bf16[3,256,256]{2,1,0:T(8,128)(2,1)S(1)} %get-tuple-element.625), channel_id=1, source_target_pairs={{0,2},{1,3},{2,0},{3,1},{4,6},{5,7},{6,4},{7,5},{8,10},{9,11},{10,... | collective-permute-start | bytes 1179656 | tf_op jit(solution)/shard_map/ppermute | solution.py:230
  383.2 17.3 %collective-permute-start.2 = (bf16[3,256,256]{2,1,0:T(8,128)(2,1)S(1)}, bf16[3,256,256]{2,1,0:T(8,128)(2,1)S(1)}, u32[]{:S(2)}, u32[]{:S(2)}) collective-permute-start(bf16[3,256,256]{2,1,0:T(8,128)(2,1)S(1)} %get-tuple-element.624), channel_id=1, source_target_pairs={{0,3},{1,0},{2,1},{3,2},{4,7},{5,4},{6,5},{7,6},{8,11},{9,8},{10,9... | collective-permute-start | bytes 1179656 | tf_op jit(solution)/shard_map/ppermute | solution.py:230
  414.9 131.4 %reduce-scatter.3.cloned.1.call-start = ((), (), s32[]{:S(2)}) async-start(), calls=%async_computation.7 | async-start | bytes 4456448 | tf_op jit(solution)/shard_map/reduce_scatter | solution.py:262
Sparse Core Ops, SparseCore 0:
  9.6 31.2 all-gather.11
  48.7 35.6 all-gather.13
  219.1 37.0 all-gather.19
  296.8 37.2 all-gather.17
  335.5 21.4 all-gather.15
  415.0 54.9 reduce-scatter.4
  474.9 71.3 reduce-scatter.2
